TPU v7x, 32 devices: a whole 2x2x4 slice. The times are simulated.
32 devices in a mesh: ctx: 2 (over y), ch: 16 (over z, x, core).
Axes of the slice: x: 2, y: 2, z: 4, core: 2. Of those that a mesh axis runs over, the one named last changes fastest.
Arguments:
- projections: bfloat16 [4, 1024, 3, 4096], P(None, ('ctx', 'ch')), may hold values from -6 to 6
- impulse: float32 [1024, 4096], P('ctx', 'ch'), may hold values from -4 to 4, as said below
- skip_gain: float32 [4096], P('ch'), may hold values from 0.3 to 1.5
Outputs:
- gated: bfloat16 [4, 1024, 4096], P(None, ('ctx', 'ch'))
Inputs may be any that keep to these rules, and one draw needn't show every extreme that they name: impulse holds a filter of each channel over lags.
All inputs are finite; a program needn't handle non-finite values.
Results may differ from a plain program's by a relative error of at most 0.0056.
Values may be sent and summed in bfloat16 or wider, within the bound.
A program may use at most 128 MiB of HBM per device.

v0:
```python
import math

import jax
import jax.numpy as jnp
from jax import lax
from jax.sharding import PartitionSpec as P


def passed_along(value, axis, steps):
    count = lax.axis_size(axis)
    leading, last = (max(0, -steps), min(count, count - steps))
    return lax.ppermute(value, axis, [(source, source + steps) for source in range(leading, last)])


def forward_table(length):
    frequency = lax.broadcasted_iota(jnp.int32, (length, length), 0)
    sample = lax.broadcasted_iota(jnp.int32, (length, length), 1)
    angles = (frequency * sample % (2 * length)).astype(jnp.float32) * (math.pi / length)
    nyquist = jnp.where(sample % 2 == 0, jnp.float32(1.0), jnp.float32(-1.0))
    packed_imag = jnp.where(frequency == 0, nyquist, -jnp.sin(angles))
    return jnp.stack([jnp.cos(angles), packed_imag], axis=0)


def inverse_table(length):
    sample = lax.broadcasted_iota(jnp.int32, (2 * length, length), 0)
    frequency = lax.broadcasted_iota(jnp.int32, (2 * length, length), 1)
    angles = (frequency * sample % (2 * length)).astype(jnp.float32) * (math.pi / length)
    weight = jnp.where(frequency == 0, jnp.float32(0.5), jnp.float32(1.0)) / length
    nyquist = jnp.where(sample % 2 == 0, jnp.float32(0.5), jnp.float32(-0.5)) / length
    imag_part = jnp.where(frequency == 0, nyquist, -weight * jnp.sin(angles))
    return jnp.stack([weight * jnp.cos(angles), imag_part], axis=1)


def spectral_product(left_side, right_side):
    left_real = left_side[..., 0, :, :]
    left_imag = left_side[..., 1, :, :]
    right_real = right_side[..., 0, :, :]
    right_imag = right_side[..., 1, :, :]
    first_bin = lax.broadcasted_iota(jnp.int32, (left_real.shape[-2], 1), 0) == 0
    real_part = jnp.where(
        first_bin, left_real * right_real, left_real * right_real - left_imag * right_imag
    )
    imag_part = jnp.where(
        first_bin, left_imag * right_imag, left_real * right_imag + left_imag * right_real
    )
    return jnp.stack([real_part, imag_part], axis=-3)


def body(projections, impulse, skip_gain):
    length = impulse.shape[0]
    blocks = lax.axis_size("ctx")
    position = lax.axis_index("ctx")
    forward = forward_table(length)
    forward_low = forward.astype(jnp.bfloat16)
    received = lax.all_to_all(projections, "ch", split_axis=3, concat_axis=1, tiled=True)
    gate_part = received[:, :, 0, :]
    mixed_input = (
        received[:, :, 1, :].astype(jnp.float32) * received[:, :, 2, :].astype(jnp.float32)
    ).astype(jnp.bfloat16)
    spectrum, mixed_input, gate_rows = (
        jnp.einsum(
            "pkn,snc->spkc", forward_low, mixed_input, preferred_element_type=jnp.float32
        ).astype(jnp.bfloat16),
        mixed_input,
        gate_part,
    )
    own_filter = jnp.einsum("pkn,nc->pkc", forward, impulse, precision=lax.Precision.HIGHEST)
    filters = lax.all_gather(own_filter[None], "ctx", axis=0, tiled=True)
    zero_carry = jnp.zeros(spectrum.shape, jnp.float32)
    pieces = lax.all_gather(spectrum[None], "ctx", axis=0, tiled=True)
    current = zero_carry
    previous = zero_carry
    for offset in range(pieces.shape[0]):
        source = pieces[offset].astype(jnp.float32)
        lag_index = position - offset
        chosen = lax.dynamic_index_in_dim(
            filters, jnp.clip(lag_index, 0, blocks - 1), 0, keepdims=False
        )
        weight = (lag_index >= 0).astype(jnp.float32)
        current = current + spectral_product(source, chosen) * weight
    current, previous = (current, previous)
    inverse = inverse_table(length)
    signal = jnp.einsum("npk,spkc->snc", inverse, current, precision=lax.Precision.HIGHEST)
    head_part = signal[:, :length]
    tail_part = passed_along(signal[:, length:], "ctx", 1)
    mixed_wide = lax.optimization_barrier(mixed_input).astype(jnp.float32)
    convolved = head_part + tail_part + skip_gain * mixed_wide
    gated = (gate_rows.astype(jnp.float32) * convolved).astype(jnp.bfloat16)
    return lax.all_to_all(gated, "ch", split_axis=1, concat_axis=2, tiled=True)


def solution(mesh):
    return jax.shard_map(
        body,
        mesh=mesh,
        in_specs=(P(None, ("ctx", "ch"), None, None), P("ctx", "ch"), P("ch")),
        out_specs=P(None, ("ctx", "ch"), None),
        check_vma=False,
    )
```

profile of v0, /device:TPU:0, one launch (start us, length us, event | category | flops | bytes accessed | tf_op | source)
XLA Modules:
  0.0 349.0 jit_solution(7590995391529949051)
XLA Ops:
  6.5 16.6 %copy.33 = bf16[4,32,3,4096]{1,0,2,3:T(4,128)(2,1)} copy(bf16[4,32,3,4096]{3,1,2,0:T(8,128)(2,1)} %param.3) | data formatting | bytes 6291456 | tf_op args[0]
  23.1 17.7 %reshape.390 = bf16[16,2,49152]{2,1,0:T(2,128)(2,1)} reshape(bf16[4096,3,4,32]{3,2,1,0:T(4,128)(2,1)} %bitcast.50) | data formatting | bytes 6291456
  40.8 7.4 %all-to-all-start = ((bf16[16,2,49152]{2,1,0:T(2,128)(2,1)}), bf16[16,2,49152]{2,1,0:T(2,128)(2,1)}, u32[]{:S(2)}, u32[]{:S(2)}) async-start(bf16[16,2,49152]{2,1,0:T(2,128)(2,1)} %reshape.390), calls=%async_computation | async-start | bytes 6291456 | tf_op jit(solution)/shard_map/all_to_all | solution.py:55
  48.3 3.8 %fusion.35 = f32[1,512,512]{2,1,0:T(8,128)S(1)} fusion(), kind=kLoop, calls=%fused_computation.61 | loop fusion | flops 3670016 | bytes 1048576 | tf_op jit(solution)/shard_map/cos | solution.py:21
  52.1 4.0 %negate_select_fusion.4 = f32[1,512,512]{2,1,0:T(8,128)S(1)} fusion(s32[512]{0:T(512)S(1)} %get-tuple-element.22, s32[512]{0:T(512)S(1)} %get-tuple-element.23, pred[512]{0:T(512)(128)(4,1)S(1)} %get-tuple-element.24, pred[512]{0:T(512)(128)(4,1)S(1)} %get-tuple-element.25), kind=kLoop, calls=%fused_computation.51 | loop fusion | flops 4980736 | bytes 1053696 | tf_op jit(solution)/shard_map/jit(_where)/select_n | solution.py:20
  57.0 2.8 fusion.23
  60.1 47.5 %all-to-all-done = bf16[16,2,49152]{2,1,0:T(2,128)(2,1)} async-done(((bf16[16,2,49152]{2,1,0:T(2,128)(2,1)}), bf16[16,2,49152]{2,1,0:T(2,128)(2,1)}, u32[]{:S(2)}, u32[]{:S(2)}) %all-to-all-start) | async-done | bytes 3145760 | tf_op jit(solution)/shard_map/all_to_all | solution.py:55
  107.6 14.5 %reshape.391 = bf16[4096,3,4,32]{3,2,1,0:T(4,128)(2,1)} reshape(bf16[16,2,49152]{2,1,0:T(2,128)(2,1)} %all-to-all-done) | data formatting | bytes 6291456
  122.1 17.7 %copy.48 = bf16[4,32,3,16,256]{4,1,3,2,0:T(8,128)(2,1)} copy(bf16[4,32,3,16,256]{1,0,2,4,3:T(4,128)(2,1)} %bitcast.49) | data formatting | bytes 6291456 | tf_op jit(solution)/shard_map/all_to_all | solution.py:55
  139.8 3.4 fusion.49
  145.2 4.2 %convert_bitcast_fusion = bf16[4,2,512,256]{2,3,1,0:T(8,128)(2,1)} fusion(f32[1,512,512]{2,1,0:T(8,128)} %copy-done.3, f32[1,512,512]{2,1,0:T(8,128)} %copy-done.2, bf16[4,512,1,256]{1,3,0,2:T(8,128)(2,1)S(1)} %copy.51, bf16[4,512,1,256]{1,3,0,2:T(8,128)(2,1)S(1)} %copy.50), kind=kOutput, calls=%fused_computation.36 | convolution fusion | flops 1078984704 | bytes 6291456 | tf_op jit(solution)/shard_map/pkn,snc->spkc/dot_general | solution.py:61
  149.4 4.2 %copy.39 = bf16[4,2,512,256]{3,2,1,0:T(8,128)(2,1)} copy(bf16[4,2,512,256]{2,3,1,0:T(8,128)(2,1)} %convert_bitcast_fusion) | data formatting | bytes 4194304 | tf_op jit(solution)/shard_map/convert_element_type | solution.py:63
  153.7 8.6 %cosine_multiply_fusion = f32[1024,1,512]{2,0,1:T(8,128)} fusion(f32[512]{0:T(512)S(1)} %select_multiply_fusion), kind=kLoop, calls=%fused_computation.29 | loop fusion | flops 7864320 | bytes 2099200 | tf_op jit(solution)/shard_map/mul | solution.py:31
  162.3 9.0 %multiply_select_fusion = f32[1024,1,512]{2,0,1:T(8,128)} fusion(f32[512]{0:T(512)S(1)} %fusion.45, s32[1024]{0:T(1024)S(1)} %get-tuple-element.20, s32[1024]{0:T(1024)S(1)} %get-tuple-element.21, pred[1024]{0:T(1024)(128)(4,1)S(1)} %fusion.40, pred[512]{0:T(512)(128)(4,1)S(1)} %get-tuple-element.24), kind=kLoop, calls=%fused_computation.27 | loop fusion | flops 10485760 | bytes 2108928 | tf_op jit(solution)/shard_map/jit(_where)/select_n | solution.py:30
  171.3 3.0 dynamic-slice_bitcast_fusion.1
  174.3 47.0 %all-gather.5.cloned.1.call-done = bf16[8,2,512,256]{3,2,1,0:T(8,128)(2,1)} async-done(((bf16[4,2,512,256]{3,2,1,0:T(8,128)(2,1)}), bf16[8,2,512,256]{3,2,1,0:T(8,128)(2,1)}) %all-gather.5.cloned.1.call-update) | async-done | bytes 4194320 | tf_op jit(solution)/shard_map/all_gather | solution.py:70
  221.3 3.2 slice_convert_fusion
  226.8 27.5 %fusion.9 = f32[4,1024,256]{1,2,0:T(8,128)S(1)} fusion(f32[1024,1,512]{2,0,1:T(8,128)S(1)} %copy-done.8, f32[1024,1,512]{2,0,1:T(8,128)S(1)} %copy-done.9, f32[4,1,512,256]{3,2,1,0:T(8,128)S(1)} %get-tuple-element.18, f32[4,1,512,256]{3,2,1,0:T(8,128)S(1)} %get-tuple-element.19, f32[4,1,512,256]{3,2,1,0:T(8,128)S(1)} %get-tuple-element.6, ...), kind=kOutput, calls=%fused_computation.16 | convolution fusion | flops 12891193344 | bytes 16777224 | tf_op jit(solution)/shard_map/npk,spkc->snc/dot_general | solution.py:83
  254.3 1.7 slice.76
  257.0 3.7 %collective-permute-start = (f32[4,512,256]{1,2,0:T(8,128)}, f32[4,512,256]{1,2,0:T(8,128)}, u32[]{:S(2)}, u32[]{:S(2)}) collective-permute-start(f32[4,512,256]{1,2,0:T(8,128)} %slice.76), channel_id=1, source_target_pairs={{0,16},{1,17},{2,18},{3,19},{4,20},{5,21},{6,22},{7,23},{8,24},{9,... | collective-permute-start | bytes 6291464 | tf_op jit(solution)/shard_map/ppermute | solution.py:12
  263.6 41.1 %collective-permute-done = f32[4,512,256]{1,2,0:T(8,128)} collective-permute-done((f32[4,512,256]{1,2,0:T(8,128)}, f32[4,512,256]{1,2,0:T(8,128)}, u32[]{:S(2)}, u32[]{:S(2)}) %collective-permute-start) | collective-permute-done | bytes 2097184 | tf_op jit(solution)/shard_map/ppermute | solution.py:12
  304.7 4.0 %fusion.17 = bf16[4,512,256]{1,2,0:T(8,128)(2,1)} fusion(f32[4,512,256]{1,2,0:T(8,128)} %collective-permute-done, f32[4,1024,256]{1,2,0:T(8,128)} %copy-done.5, bf16[4,512,256]{1,2,0:T(8,128)(2,1)S(1)} %copy-done.4, bf16[4,512,1,256]{1,3,0,2:T(8,128)(2,1)S(1)} %copy.49, f32[256]{0:T(256)S(1)} %copy-done.10), kind=kLoop, calls=%fused_computation.23 | loop fusion | flops 3670016 | bytes 7341056 | tf_op jit(solution)/shard_map/convert_element_type | solution.py:88
  308.8 1.7 copy.41
  310.4 30.5 %all_to_all.36 = bf16[4,512,256]{2,0,1:T(4,128)(2,1)S(1)} all-to-all(bf16[4,512,256]{2,0,1:T(4,128)(2,1)S(1)} %copy.41), channel_id=1, replica_groups=mesh['ctx'=2,'ch'=16] {'ch'}, dimensions={1} | all-to-all | bytes 2097152 | tf_op jit(solution)/shard_map/all_to_all | solution.py:89
  (40 shorter events, 10.6 us)
Async XLA Ops:
  6.5 50.5 %copy-start = (f32[512,256]{1,0:T(8,128)S(1)}, f32[512,256]{1,0:T(8,128)}, u32[]{:S(2)}) copy-start(f32[512,256]{1,0:T(8,128)} %param.4) | copy-start | bytes 1572868
  40.8 66.8 %all-to-all-start = ((bf16[16,2,49152]{2,1,0:T(2,128)(2,1)}), bf16[16,2,49152]{2,1,0:T(2,128)(2,1)}, u32[]{:S(2)}, u32[]{:S(2)}) async-start(bf16[16,2,49152]{2,1,0:T(2,128)(2,1)} %reshape.390), calls=%async_computation | async-start | bytes 6291456 | tf_op jit(solution)/shard_map/all_to_all | solution.py:55
  48.2 123.1 %all-gather.7.cloned.1.call-start = ((), (), s32[]{:S(2)}) async-start(), calls=%async_computation.3 | async-start | bytes 3145728 | tf_op jit(solution)/shard_map/all_gather | solution.py:68
  52.0 4.0 %copy-start.2 = (f32[1,512,512]{2,1,0:T(8,128)}, f32[1,512,512]{2,1,0:T(8,128)S(1)}, u32[]{:S(2)}) copy-start(f32[1,512,512]{2,1,0:T(8,128)S(1)} %fusion.35) | copy-start | bytes 3145732
  56.1 1.0 copy-start.3
  59.8 161.5 %all-gather.5.cloned.1.call-start = ((), (), s32[]{:S(2)}) async-start(), calls=%async_computation.2 | async-start | bytes 6291456 | tf_op jit(solution)/shard_map/all_gather | solution.py:70
  221.3 3.2 copy-start.6
  221.3 3.2 copy-start.7
  224.6 1.6 copy-start.8
  224.6 2.2 copy-start.9
  254.3 2.7 copy-start.5
  257.0 47.7 %copy-start.10 = (f32[256]{0:T(256)S(1)}, f32[256]{0:T(256)}, u32[]{:S(2)}) copy-start(f32[256]{0:T(256)} %param.5) | copy-start | bytes 3076
  257.0 47.7 %collective-permute-start = (f32[4,512,256]{1,2,0:T(8,128)}, f32[4,512,256]{1,2,0:T(8,128)}, u32[]{:S(2)}, u32[]{:S(2)}) collective-permute-start(f32[4,512,256]{1,2,0:T(8,128)} %slice.76), channel_id=1, source_target_pairs={{0,16},{1,17},{2,18},{3,19},{4,20},{5,21},{6,22},{7,23},{8,24},{9,... | collective-permute-start | bytes 6291464 | tf_op jit(solution)/shard_map/ppermute | solution.py:12
  262.0 42.7 %copy-start.4 = (bf16[4,512,256]{1,2,0:T(8,128)(2,1)S(1)}, bf16[4,512,256]{1,2,0:T(8,128)(2,1)}, u32[]{:S(2)}) copy-start(bf16[4,512,256]{1,2,0:T(8,128)(2,1)} %fusion.36) | copy-start | bytes 3145732
  310.4 31.7 %copy-start.1 = (f32[512,256]{1,0:T(8,128)S(1)}, f32[512,256]{1,0:T(8,128)}, u32[]{:S(2)}) copy-start(f32[512,256]{1,0:T(8,128)} %param.4) | copy-start | bytes 1572868
Sparse Core Ops, SparseCore 0:
  60.0 34.4 all-gather.6
  153.7 67.5 all-gather.4
where the time goes:
time: 352 us; the launch traced here: 349 us
  waiting for transfers between devices  136 us (39%)
  local copies, waits for them, and re-layouts  87.9 us (25%)
  other arithmetic  35.4 us (10%)
  matrix products  34.5 us (10%)
  blocking collectives  30.5 us (9%)
  between operations  13.6 us (4%)
  starting transfers between devices  11.4 us (3%)
    unnamed x28, local copies, waits for them, and re-layouts  55.1 us
    all_to_all x1, waiting for transfers between devices, body(): lax.all_to_all(projections, 'ch', split_axis=3, concat_axis=1, tiled=True)  47.5 us
    all_gather x1, waiting for transfers between devices, body(): pieces = lax.all_gather(spectrum[None], 'ctx', axis=0, tiled=True)  47 us
    ppermute x1, waiting for transfers between devices, passed_along(): lax.ppermute(value, axis, [(source, source + steps) for source in range(l...  41.1 us
    all_to_all x1, blocking collectives, body(): return lax.all_to_all(gated, 'ch', split_axis=1, concat_axis=2, tiled=True)  30.5 us
    dot_general x1, matrix products, body(): jnp.einsum('npk,spkc->snc', inverse, current, precision=lax.Precision.HIG...  27.5 us
    all_to_all x1, local copies, waits for them, and re-layouts, body(): lax.all_to_all(projections, 'ch', split_axis=3, concat_axis=1, tiled=True)  17.7 us
    select_n x1, other arithmetic, inverse_table(): imag_part = jnp.where(frequency == 0, nyquist, -weight * jnp.sin(angles))  9 us
  transfers between devices with their start and end apart: 4, of which 3 were waited for; matrix products, arithmetic and copies ran while one was open for 23% of the time, Pallas kernels for 0%

commit v1 on v0

--- a/solution.py
+++ b/solution.py
@@ -1,9 +1,17 @@
+import functools
 import math
 
 import jax
 import jax.numpy as jnp
 from jax import lax
+from jax.experimental import pallas as pl
+from jax.experimental.pallas import tpu as pltpu
 from jax.sharding import PartitionSpec as P
+import ml_dtypes
+import numpy as np
+
+MESH = pl.DeviceIdType.MESH
+LANES = 128
 
 
 def passed_along(value, axis, steps):
@@ -46,7 +54,7 @@
     return jnp.stack([real_part, imag_part], axis=-3)
 
 
-def body(projections, impulse, skip_gain):
+def general_body(projections, impulse, skip_gain):
     length = impulse.shape[0]
     blocks = lax.axis_size("ctx")
     position = lax.axis_index("ctx")
@@ -89,6 +97,259 @@
     return lax.all_to_all(gated, "ch", split_axis=1, concat_axis=2, tiled=True)
 
 
+def split_table(length):
+    frequency = np.arange(length)[:, None]
+    sample = np.arange(length)[None, :]
+    angles = (frequency * sample % (2 * length)) * (math.pi / length)
+    nyquist = np.where(sample % 2 == 0, 1.0, -1.0)
+    imag = np.where(frequency == 0, nyquist, -np.sin(angles))
+    table = np.concatenate([np.cos(angles), imag], axis=0)
+    high = table.astype(ml_dtypes.bfloat16)
+    low = (table - high.astype(np.float64)).astype(ml_dtypes.bfloat16)
+    return high, low
+
+
+def dot(left, right):
+    return jnp.dot(left, right, preferred_element_type=jnp.float32)
+
+
+def mixer_kernel(
+    ctx_size, ch_size,
+    proj_ref, impulse_ref, skip_ref, high_ref, low_ref,
+    conv_ref,
+    kv, mixed, received, result, lags, coef, back_high, back_low, sum_high, sum_low,
+    load_sem, lag_sems, out_send, out_recv, home_send, home_recv,
+):
+    seqs, _, tokens, _ = proj_ref.shape
+    span = impulse_ref.shape[0]
+    count = ctx_size * ch_size
+    y, c = lax.axis_index("ctx"), lax.axis_index("ch")
+    me = y * ch_size + c
+    tile = 128
+    tiles = span // tile
+
+    def place(device):
+        return device // ch_size, device % ch_size
+
+    def columns(device):
+        py, pc = place(device)
+        return pl.ds(pl.multiple_of((pc * ctx_size + py) * LANES, LANES), LANES)
+
+    def rows(device):
+        return pl.ds(pl.multiple_of(device * tokens, tokens), tokens)
+
+    def peer(step):
+        return lax.rem(me + step, count)
+
+    def load(s):
+        return pltpu.make_async_copy(proj_ref.at[s, pl.ds(1, 2)], kv.at[s], load_sem.at[s])
+
+    for s in range(seqs):
+        load(s).start()
+    own_lag = pltpu.make_async_copy(
+        impulse_ref.at[:, pl.ds(pl.multiple_of(y * LANES, LANES), LANES)], lags.at[y], lag_sems.at[0]
+    )
+    own_lag.start()
+
+    barrier = pltpu.get_barrier_semaphore()
+
+    def greet(step, carry):
+        pl.semaphore_signal(barrier, inc=1, device_id=place(peer(step)), device_id_type=MESH)
+        return carry
+
+    lax.fori_loop(1, count, greet, 0)
+    pl.semaphore_wait(barrier, count - 1)
+
+    other = 1 - y
+    lag_copy = pltpu.make_async_remote_copy(
+        src_ref=impulse_ref.at[:, pl.ds(pl.multiple_of(other * LANES, LANES), LANES)],
+        dst_ref=lags.at[y],
+        send_sem=lag_sems.at[1],
+        recv_sem=lag_sems.at[2],
+        device_id=(other, c),
+        device_id_type=MESH,
+    )
+    lag_copy.start()
+
+    def send_out(s, carry):
+        load(s).wait()
+        mixed[s] = (kv[s, 0].astype(jnp.float32) * kv[s, 1].astype(jnp.float32)).astype(jnp.bfloat16)
+        pltpu.make_async_copy(
+            mixed.at[s, :, columns(me)], received.at[s, rows(me), :], out_recv.at[s]
+        ).start()
+
+        def one(step, inner):
+            target = peer(step)
+            pltpu.make_async_remote_copy(
+                src_ref=mixed.at[s, :, columns(target)],
+                dst_ref=received.at[s, rows(me), :],
+                send_sem=out_send.at[s],
+                recv_sem=out_recv.at[s],
+                device_id=place(target),
+                device_id_type=MESH,
+            ).start()
+            return inner
+
+        return lax.fori_loop(1, count, one, carry)
+
+    lax.fori_loop(0, seqs, send_out, 0)
+
+    row = lax.broadcasted_iota(jnp.int32, (span, span), 0)
+    col = lax.broadcasted_iota(jnp.int32, (span, span), 1)
+    alternating = jnp.where(row % 2 == 0, jnp.float32(1.0), jnp.float32(-1.0))
+    imag = high_ref[span:, :].astype(jnp.float32)
+    imag = jnp.where(row == 0, jnp.float32(0.0), imag)
+    back_high[:, :span] = high_ref[:span, :]
+    back_high[:, span:] = jnp.where(col == 0, alternating, imag).astype(jnp.bfloat16)
+    back_low[:, :span] = low_ref[:span, :]
+    back_low[:, span:] = low_ref[span:, :]
+
+    own_lag.wait()
+    lag_copy.wait()
+    taps = jnp.concatenate([lags[0], lags[1]], axis=1)
+    taps_high = taps.astype(jnp.bfloat16)
+    taps_low = (taps - taps_high.astype(jnp.float32)).astype(jnp.bfloat16)
+    for t in range(tiles):
+        parts = []
+        for p in range(2):
+            at = pl.ds(p * span + t * tile, tile)
+            parts.append(
+                dot(high_ref[at, :], taps_high)
+                + dot(high_ref[at, :], taps_low)
+                + dot(low_ref[at, :], taps_high)
+            )
+        real, imag = parts
+        bins = lax.broadcasted_iota(jnp.int32, (tile, LANES), 0) + t * tile
+        first = bins == 0
+        sign = jnp.where(bins % 2 == 0, jnp.float32(1.0), jnp.float32(-1.0))
+        weight = jnp.where(first, jnp.float32(0.5 / span), jnp.float32(1.0 / span))
+        re0, im0 = real[:, :LANES] * weight, imag[:, :LANES] * weight
+        re1 = real[:, LANES:] * weight + sign * re0
+        im1 = imag[:, LANES:] * weight + sign * im0
+        at = pl.ds(t * tile, tile)
+        for base, re, im in ((0, re0, im0), (3, re1, im1)):
+            coef[base, at, :] = re
+            coef[base + 1, at, :] = jnp.where(first, jnp.float32(0.0), im)
+            coef[base + 2, at, :] = jnp.where(first, im, re)
+
+    def convolve(s, carry):
+        pltpu.make_async_copy(received.at[s], received.at[s], out_recv.at[s]).wait()
+        signal = jnp.concatenate([received[s, :span, :], received[s, span:, :]], axis=1)
+        for t in range(tiles):
+            at = pl.ds(t * tile, tile)
+            re = dot(high_ref[at, :], signal).astype(jnp.bfloat16).astype(jnp.float32)
+            im = dot(high_ref[pl.ds(span + t * tile, tile), :], signal)
+            im = im.astype(jnp.bfloat16).astype(jnp.float32)
+            re0, re1 = re[:, :LANES], re[:, LANES:]
+            im0, im1 = im[:, :LANES], im[:, LANES:]
+            a0, b0, c0 = coef[0, at, :], coef[1, at, :], coef[2, at, :]
+            a1, b1, c1 = coef[3, at, :], coef[4, at, :], coef[5, at, :]
+            sums = (
+                (re0 * a0 - im0 * b0, im0 * c0 + re0 * b0),
+                (
+                    re0 * a1 - im0 * b1 + (re1 * a0 - im1 * b0),
+                    im0 * c1 + re0 * b1 + (im1 * c0 + re1 * b0),
+                ),
+            )
+            for p in range(2):
+                total = jnp.concatenate([sums[0][p], sums[1][p]], axis=1)
+                high = total.astype(jnp.bfloat16)
+                into = pl.ds(p * span + t * tile, tile)
+                sum_high[into, :] = high
+                sum_low[into, :] = (total - high.astype(jnp.float32)).astype(jnp.bfloat16)
+        gain = skip_ref[pl.ds(y, 1), :]
+        for t in range(tiles):
+            at = pl.ds(t * tile, tile)
+            response = (
+                dot(back_high[at, :], sum_high[...])
+                + dot(back_high[at, :], sum_low[...])
+                + dot(back_low[at, :], sum_high[...])
+            )
+            for j in range(2):
+                into = pl.ds(j * span + t * tile, tile)
+                direct = gain * received[s, into, :].astype(jnp.float32)
+                result[s, into, :] = (
+                    response[:, j * LANES : (j + 1) * LANES] + direct
+                ).astype(jnp.bfloat16)
+        pltpu.make_async_copy(
+            result.at[s, rows(me), :], conv_ref.at[s, :, columns(me)], home_recv.at[s]
+        ).start()
+
+        def one(step, inner):
+            target = peer(step)
+            pltpu.make_async_remote_copy(
+                src_ref=result.at[s, rows(target), :],
+                dst_ref=conv_ref.at[s, :, columns(me)],
+                send_sem=home_send.at[s],
+                recv_sem=home_recv.at[s],
+                device_id=place(target),
+                device_id_type=MESH,
+            ).start()
+            return inner
+
+        return lax.fori_loop(1, count, one, carry)
+
+    lax.fori_loop(0, seqs, convolve, 0)
+
+    def drain(s, carry):
+        sent = received.at[s, pl.ds(0, (count - 1) * tokens), :]
+        pltpu.make_async_copy(sent, sent, out_send.at[s]).wait()
+        pltpu.make_async_copy(sent, sent, home_send.at[s]).wait()
+        pltpu.make_async_copy(conv_ref.at[s], conv_ref.at[s], home_recv.at[s]).wait()
+        return carry
+
+    lax.fori_loop(0, seqs, drain, 0)
+
+
+def split_body(projections, impulse, skip_gain):
+    ctx_size, ch_size = lax.axis_size("ctx"), lax.axis_size("ch")
+    seqs, tokens, _, width = projections.shape
+    span = impulse.shape[0]
+    length = ctx_size * ch_size * tokens
+    high, low = split_table(span)
+    features = jnp.transpose(projections, (0, 2, 1, 3))
+    anywhere = pl.BlockSpec(memory_space=pl.ANY)
+    vmem = pl.BlockSpec(memory_space=pltpu.VMEM)
+    bf16, f32 = jnp.bfloat16, jnp.float32
+    convolved = pl.pallas_call(
+        functools.partial(mixer_kernel, ctx_size, ch_size),
+        out_shape=jax.ShapeDtypeStruct((seqs, tokens, width), bf16),
+        in_specs=[anywhere, anywhere, vmem, vmem, vmem],
+        out_specs=anywhere,
+        scratch_shapes=[
+            pltpu.VMEM((seqs, 2, tokens, width), bf16),
+            pltpu.VMEM((seqs, tokens, width), bf16),
+            pltpu.VMEM((seqs, length, LANES), bf16),
+            pltpu.VMEM((seqs, length, LANES), bf16),
+            pltpu.VMEM((2, span, LANES), f32),
+            pltpu.VMEM((6, span, LANES), f32),
+            pltpu.VMEM((span, 2 * span), bf16),
+            pltpu.VMEM((span, 2 * span), bf16),
+            pltpu.VMEM((2 * span, 2 * LANES), bf16),
+            pltpu.VMEM((2 * span, 2 * LANES), bf16),
+            pltpu.SemaphoreType.DMA((seqs,)),
+            pltpu.SemaphoreType.DMA((3,)),
+            pltpu.SemaphoreType.DMA((seqs,)),
+            pltpu.SemaphoreType.DMA((seqs,)),
+            pltpu.SemaphoreType.DMA((seqs,)),
+            pltpu.SemaphoreType.DMA((seqs,)),
+        ],
+        compiler_params=pltpu.CompilerParams(
+            collective_id=0, has_side_effects=True, vmem_limit_bytes=40 * 1024 * 1024
+        ),
+    )(features, impulse, skip_gain.reshape(2, LANES), jnp.asarray(high), jnp.asarray(low))
+    gate = features[:, 0]
+    return (gate.astype(f32) * convolved.astype(f32)).astype(bf16)
+
+
+def body(projections, impulse, skip_gain):
+    ctx_size = lax.axis_size("ctx")
+    whole_tiles = projections.shape[1] % 16 == 0 and impulse.shape[0] % 256 == 0
+    if ctx_size == 2 and impulse.shape[1] == 2 * LANES and whole_tiles:
+        return split_body(projections, impulse, skip_gain)
+    return general_body(projections, impulse, skip_gain)
+
+
 def solution(mesh):
     return jax.shard_map(
         body,

time: 352 us -> 60.7 us (0.17)
  waiting for transfers between devices: 136 us -> 0 us
  local copies, waits for them, and re-layouts: 87.9 us -> 6.06 us
  Pallas kernels: 0 us -> 53.2 us
  matrix products: 34.5 us -> 0 us
  other arithmetic: 35.4 us -> 1.22 us
  blocking collectives: 30.5 us -> 0 us
  between operations: 13.6 us -> 0.01 us
  starting transfers between devices: 11.4 us -> 0 us
    pallas_call x0 -> x1, Pallas kernels: none -> 53.2 us  [split_body(): pl.pallas_call(functools.partial(mixer_kernel, ctx_size, ch_size), out_sh...]
    unnamed x28 -> x10, local copies, waits for them, and re-layouts: 55.1 us -> 6.06 us
    all_to_all x1 -> x0, waiting for transfers between devices: 47.5 us -> none  [body(): lax.all_to_all(projections, 'ch', split_axis=3, concat_axis=1, tiled=True)]
    all_gather x2 -> x0, waiting for transfers between devices: 47 us -> none  [the longest x1 47 us: body(): pieces = lax.all_gather(spectrum[None], 'ctx', axis=0, tiled=True)]
    ppermute x1 -> x0, waiting for transfers between devices: 41.1 us -> none  [passed_along(): lax.ppermute(value, axis, [(source, source + steps) for source in range(l...]
    dot_general x3 -> x0, matrix products: 34.5 us -> none  [the longest x1 27.5 us: body(): jnp.einsum('npk,spkc->snc', inverse, current, precision=lax.Precision.HIG...]
    all_to_all x1 -> x0, blocking collectives: 30.5 us -> none  [body(): return lax.all_to_all(gated, 'ch', split_axis=1, concat_axis=2, tiled=True)]
    all_to_all x3 -> x0, local copies, waits for them, and re-layouts: 18.9 us -> none  [the longest x1 17.7 us: body(): lax.all_to_all(projections, 'ch', split_axis=3, concat_axis=1, tiled=True)]
  transfers between devices with their start and end apart: 4 -> 0, of which waited for: 3 -> 0; matrix products, arithmetic and copies ran while one was open for 23% -> 0% of each run, Pallas kernels for 0% -> 0%
where the time goes in v1:
time: 60.7 us; the launch traced here: 60.5 us
  Pallas kernels  53.2 us (88%)
  local copies, waits for them, and re-layouts  6.06 us (10%)
  other arithmetic  1.22 us (2%)
    pallas_call x1, Pallas kernels, split_body(): pl.pallas_call(functools.partial(mixer_kernel, ctx_size, ch_size), out_sh...  53.2 us
    unnamed x10, local copies, waits for them, and re-layouts  6.06 us
    convert_element_type x1, other arithmetic, split_body(): return (gate.astype(f32) * convolved.astype(f32)).astype(bf16)  1.22 us

profile of v1, /device:TPU:0, one launch (start us, length us, event | category | flops | bytes accessed | tf_op | source)
XLA Modules:
  0.0 60.5 jit_solution(9507653305691378831)
XLA Ops:
  0.0 0.0 copy-start
  0.0 1.9 %copy-done = bf16[4,32,3,4096]{3,1,2,0:T(8,128)(2,1)S(1)} copy-done((bf16[4,32,3,4096]{3,1,2,0:T(8,128)(2,1)S(1)}, bf16[4,32,3,4096]{3,1,2,0:T(8,128)(2,1)}, u32[]{:S(2)}) %copy-start) | copy-done | bytes 3145752
  1.9 0.0 copy-start.1
  1.9 1.2 %copy-done.1 = bf16[1024,512]{1,0:T(8,128)(2,1)S(1)} copy-done((bf16[1024,512]{1,0:T(8,128)(2,1)S(1)}, bf16[1024,512]{1,0:T(8,128)(2,1)}, u32[]{:S(2)}) %copy-start.1) | copy-done | bytes 1048600
  3.1 0.0 copy-start.2
  3.1 1.2 %copy-done.2 = bf16[1024,512]{1,0:T(8,128)(2,1)S(1)} copy-done((bf16[1024,512]{1,0:T(8,128)(2,1)S(1)}, bf16[1024,512]{1,0:T(8,128)(2,1)}, u32[]{:S(2)}) %copy-start.2) | copy-done | bytes 1048600
  4.3 0.0 copy-start.3
  4.3 1.0 %copy-done.3 = f32[512,256]{1,0:T(8,128)S(1)} copy-done((f32[512,256]{1,0:T(8,128)S(1)}, f32[512,256]{1,0:T(8,128)}, u32[]{:S(2)}) %copy-start.3) | copy-done | bytes 524312
  5.4 0.0 copy-start.4
  5.4 0.7 %copy-done.4 = f32[256]{0:T(256)S(1)} copy-done((f32[256]{0:T(256)S(1)}, f32[256]{0:T(256)}, u32[]{:S(2)}) %copy-start.4) | copy-done | bytes 1048
  6.1 53.2 %shard_map.55 = bf16[4,32,4096]{2,1,0:T(8,128)(2,1)S(1)} custom-call(bf16[4,3,32,4096]{3,2,1,0:T(8,128)(2,1)S(1)} %bitcast.7, f32[512,256]{1,0:T(8,128)S(1)} %copy-done.3, f32[2,128]{1,0:T(2,128)S(1)} %bitcast.9, bf16[1024,512]{1,0:T(8,128)(2,1)S(1)} %copy-done.2, bf16[1024,512]{1,0:T(8,128)(2,1)S(1)} %copy-done.1), custom_call_target="tpu_custom_call" | custom-call | tf_op jit(solution)/shard_map/pallas_call | solution.py:314
  59.2 1.2 %fusion = bf16[4,32,4096]{2,1,0:T(8,128)(2,1)} fusion(bf16[4,32,4096]{2,1,0:T(8,128)(2,1)S(1)} %shard_map.55, bf16[4,3,32,4096]{3,2,1,0:T(8,128)(2,1)S(1)} %bitcast.8), kind=kLoop, calls=%fused_computation.1 | loop fusion | flops 2097152 | bytes 3145728 | tf_op jit(solution)/shard_map/convert_element_type | solution.py:342
Async XLA Ops:
  0.0 1.9 %copy-start = (bf16[4,32,3,4096]{3,1,2,0:T(8,128)(2,1)S(1)}, bf16[4,32,3,4096]{3,1,2,0:T(8,128)(2,1)}, u32[]{:S(2)}) copy-start(bf16[4,32,3,4096]{3,1,2,0:T(8,128)(2,1)} %param.5) | copy-start | bytes 9437188
  1.9 1.2 %copy-start.1 = (bf16[1024,512]{1,0:T(8,128)(2,1)S(1)}, bf16[1024,512]{1,0:T(8,128)(2,1)}, u32[]{:S(2)}) copy-start(bf16[1024,512]{1,0:T(8,128)(2,1)} %constant.5.clone.low_ref) | copy-start | bytes 3145732
  3.1 1.2 %copy-start.2 = (bf16[1024,512]{1,0:T(8,128)(2,1)S(1)}, bf16[1024,512]{1,0:T(8,128)(2,1)}, u32[]{:S(2)}) copy-start(bf16[1024,512]{1,0:T(8,128)(2,1)} %constant.4.clone.high_ref) | copy-start | bytes 3145732
  4.3 1.0 %copy-start.3 = (f32[512,256]{1,0:T(8,128)S(1)}, f32[512,256]{1,0:T(8,128)}, u32[]{:S(2)}) copy-start(f32[512,256]{1,0:T(8,128)} %impulse_ref.1) | copy-start | bytes 1572868
  5.4 0.7 %copy-start.4 = (f32[256]{0:T(256)S(1)}, f32[256]{0:T(256)}, u32[]{:S(2)}) copy-start(f32[256]{0:T(256)} %param.7) | copy-start | bytes 3076

commit v2 on v1

--- a/solution.py
+++ b/solution.py
@@ -115,10 +115,10 @@
 
 def mixer_kernel(
     ctx_size, ch_size,
-    proj_ref, impulse_ref, skip_ref, high_ref, low_ref,
+    proj_ref, impulse_ref, skip_ref, high_hbm, low_hbm,
     conv_ref,
-    kv, mixed, received, result, lags, coef, back_high, back_low, sum_high, sum_low,
-    load_sem, lag_sems, out_send, out_recv, home_send, home_recv,
+    high_ref, low_ref,    kv, mixed, received, result, lags, coef, back_high, back_low, sum_high, sum_low,
+    load_sem, table_sems, lag_sems, out_send, out_recv, home_send, home_recv,
 ):
     seqs, _, tokens, _ = proj_ref.shape
     span = impulse_ref.shape[0]
@@ -126,6 +126,8 @@
     y, c = lax.axis_index("ctx"), lax.axis_index("ch")
     me = y * ch_size + c
     tile = 128
+    several = 2 if seqs % 2 == 0 else 1
+    groups = seqs // several
     tiles = span // tile
 
     def place(device):
@@ -141,8 +143,19 @@
     def peer(step):
         return lax.rem(me + step, count)
 
+    def group(g):
+        return pl.ds(g * several, several)
+
     def load(s):
         return pltpu.make_async_copy(proj_ref.at[s, pl.ds(1, 2)], kv.at[s], load_sem.at[s])
+
+    barrier = pltpu.get_barrier_semaphore()
+
+    def greet(step, carry):
+        pl.semaphore_signal(barrier, inc=1, device_id=place(peer(step)), device_id_type=MESH)
+        return carry
+
+    lax.fori_loop(1, count, greet, 0)
 
     for s in range(seqs):
         load(s).start()
@@ -150,14 +163,20 @@
         impulse_ref.at[:, pl.ds(pl.multiple_of(y * LANES, LANES), LANES)], lags.at[y], lag_sems.at[0]
     )
     own_lag.start()
-
-    barrier = pltpu.get_barrier_semaphore()
-
-    def greet(step, carry):
-        pl.semaphore_signal(barrier, inc=1, device_id=place(peer(step)), device_id_type=MESH)
+    tables = [
+        pltpu.make_async_copy(source, target, table_sems.at[i])
+        for i, (source, target) in enumerate(((high_hbm, high_ref), (low_hbm, low_ref)))
+    ]
+    for table in tables:
+        table.start()
+
+    def multiply(s, carry):
+        load(s).wait()
+        mixed[s] = (kv[s, 0].astype(jnp.float32) * kv[s, 1].astype(jnp.float32)).astype(jnp.bfloat16)
         return carry
 
-    lax.fori_loop(1, count, greet, 0)
+    lax.fori_loop(0, seqs, multiply, 0)
+
     pl.semaphore_wait(barrier, count - 1)
 
     other = 1 - y
@@ -169,22 +188,18 @@
         device_id=(other, c),
         device_id_type=MESH,
     )
-    lag_copy.start()
-
-    def send_out(s, carry):
-        load(s).wait()
-        mixed[s] = (kv[s, 0].astype(jnp.float32) * kv[s, 1].astype(jnp.float32)).astype(jnp.bfloat16)
+    def send_out(g, carry):
         pltpu.make_async_copy(
-            mixed.at[s, :, columns(me)], received.at[s, rows(me), :], out_recv.at[s]
+            mixed.at[group(g), :, columns(me)], received.at[group(g), rows(me), :], out_recv.at[g]
         ).start()
 
         def one(step, inner):
             target = peer(step)
             pltpu.make_async_remote_copy(
-                src_ref=mixed.at[s, :, columns(target)],
-                dst_ref=received.at[s, rows(me), :],
-                send_sem=out_send.at[s],
-                recv_sem=out_recv.at[s],
+                src_ref=mixed.at[group(g), :, columns(target)],
+                dst_ref=received.at[group(g), rows(me), :],
+                send_sem=out_send.at[g],
+                recv_sem=out_recv.at[g],
                 device_id=place(target),
                 device_id_type=MESH,
             ).start()
@@ -192,7 +207,11 @@
 
         return lax.fori_loop(1, count, one, carry)
 
-    lax.fori_loop(0, seqs, send_out, 0)
+    send_out(0, 0)
+    lag_copy.start()
+    lax.fori_loop(1, groups, send_out, 0)
+    for table in tables:
+        table.wait()
 
     row = lax.broadcasted_iota(jnp.int32, (span, span), 0)
     col = lax.broadcasted_iota(jnp.int32, (span, span), 1)
@@ -233,7 +252,6 @@
             coef[base + 2, at, :] = jnp.where(first, im, re)
 
     def convolve(s, carry):
-        pltpu.make_async_copy(received.at[s], received.at[s], out_recv.at[s]).wait()
         signal = jnp.concatenate([received[s, :span, :], received[s, span:, :]], axis=1)
         for t in range(tiles):
             at = pl.ds(t * tile, tile)
@@ -271,17 +289,23 @@
                 result[s, into, :] = (
                     response[:, j * LANES : (j + 1) * LANES] + direct
                 ).astype(jnp.bfloat16)
+        return carry
+
+    def send_home(g, carry):
+        landed = received.at[group(g)]
+        pltpu.make_async_copy(landed, landed, out_recv.at[g]).wait()
+        lax.fori_loop(g * several, (g + 1) * several, convolve, carry)
         pltpu.make_async_copy(
-            result.at[s, rows(me), :], conv_ref.at[s, :, columns(me)], home_recv.at[s]
+            result.at[group(g), rows(me), :], conv_ref.at[group(g), :, columns(me)], home_recv.at[g]
         ).start()
 
         def one(step, inner):
             target = peer(step)
             pltpu.make_async_remote_copy(
-                src_ref=result.at[s, rows(target), :],
-                dst_ref=conv_ref.at[s, :, columns(me)],
-                send_sem=home_send.at[s],
-                recv_sem=home_recv.at[s],
+                src_ref=result.at[group(g), rows(target), :],
+                dst_ref=conv_ref.at[group(g), :, columns(me)],
+                send_sem=home_send.at[g],
+                recv_sem=home_recv.at[g],
                 device_id=place(target),
                 device_id_type=MESH,
             ).start()
@@ -289,16 +313,17 @@
 
         return lax.fori_loop(1, count, one, carry)
 
-    lax.fori_loop(0, seqs, convolve, 0)
-
-    def drain(s, carry):
-        sent = received.at[s, pl.ds(0, (count - 1) * tokens), :]
-        pltpu.make_async_copy(sent, sent, out_send.at[s]).wait()
-        pltpu.make_async_copy(sent, sent, home_send.at[s]).wait()
-        pltpu.make_async_copy(conv_ref.at[s], conv_ref.at[s], home_recv.at[s]).wait()
+    lax.fori_loop(0, groups, send_home, 0)
+
+    def drain(g, carry):
+        sent = received.at[group(g), pl.ds(0, (count - 1) * tokens), :]
+        home = conv_ref.at[group(g)]
+        pltpu.make_async_copy(sent, sent, out_send.at[g]).wait()
+        pltpu.make_async_copy(sent, sent, home_send.at[g]).wait()
+        pltpu.make_async_copy(home, home, home_recv.at[g]).wait()
         return carry
 
-    lax.fori_loop(0, seqs, drain, 0)
+    lax.fori_loop(0, groups, drain, 0)
 
 
 def split_body(projections, impulse, skip_gain):
@@ -309,14 +334,17 @@
     high, low = split_table(span)
     features = jnp.transpose(projections, (0, 2, 1, 3))
     anywhere = pl.BlockSpec(memory_space=pl.ANY)
+    hbm = pl.BlockSpec(memory_space=pltpu.HBM)
     vmem = pl.BlockSpec(memory_space=pltpu.VMEM)
     bf16, f32 = jnp.bfloat16, jnp.float32
     convolved = pl.pallas_call(
         functools.partial(mixer_kernel, ctx_size, ch_size),
         out_shape=jax.ShapeDtypeStruct((seqs, tokens, width), bf16),
-        in_specs=[anywhere, anywhere, vmem, vmem, vmem],
+        in_specs=[hbm, hbm, vmem, hbm, hbm],
         out_specs=anywhere,
         scratch_shapes=[
+            pltpu.VMEM((2 * span, span), bf16),
+            pltpu.VMEM((2 * span, span), bf16),
             pltpu.VMEM((seqs, 2, tokens, width), bf16),
             pltpu.VMEM((seqs, tokens, width), bf16),
             pltpu.VMEM((seqs, length, LANES), bf16),
@@ -328,6 +356,7 @@
             pltpu.VMEM((2 * span, 2 * LANES), bf16),
             pltpu.VMEM((2 * span, 2 * LANES), bf16),
             pltpu.SemaphoreType.DMA((seqs,)),
+            pltpu.SemaphoreType.DMA((2,)),
             pltpu.SemaphoreType.DMA((3,)),
             pltpu.SemaphoreType.DMA((seqs,)),
             pltpu.SemaphoreType.DMA((seqs,)),
@@ -335,7 +364,7 @@
             pltpu.SemaphoreType.DMA((seqs,)),
         ],
         compiler_params=pltpu.CompilerParams(
-            collective_id=0, has_side_effects=True, vmem_limit_bytes=40 * 1024 * 1024
+            collective_id=0, has_side_effects=True, vmem_limit_bytes=60 * 1024 * 1024
         ),
     )(features, impulse, skip_gain.reshape(2, LANES), jnp.asarray(high), jnp.asarray(low))
     gate = features[:, 0]

time: 60.7 us -> 55.4 us (0.913)
  local copies, waits for them, and re-layouts: 6.06 us -> 0 us
  other arithmetic: 1.22 us -> 2.76 us
  Pallas kernels: 53.2 us -> 52.4 us
    unnamed x10 -> x0, local copies, waits for them, and re-layouts: 6.06 us -> none
    convert_element_type x1, other arithmetic: 1.22 us -> 2.76 us  [split_body(): return (gate.astype(f32) * convolved.astype(f32)).astype(bf16)]
    pallas_call x1, Pallas kernels: 53.2 us -> 52.4 us  [split_body(): pl.pallas_call(functools.partial(mixer_kernel, ctx_size, ch_size), out_sh...]
where the time goes in v2:
time: 55.4 us; the launch traced here: 55.2 us
  Pallas kernels  52.4 us (95%)
  other arithmetic  2.76 us (5%)
    pallas_call x1, Pallas kernels, split_body(): pl.pallas_call(functools.partial(mixer_kernel, ctx_size, ch_size), out_sh...  52.4 us
    convert_element_type x1, other arithmetic, split_body(): return (gate.astype(f32) * convolved.astype(f32)).astype(bf16)  2.76 us

profile of v2, /device:TPU:0, one launch (start us, length us, event | category | flops | bytes accessed | tf_op | source)
XLA Modules:
  0.0 55.2 jit_solution(186739434425173579)
XLA Ops:
  0.0 52.4 %shard_map.55 = bf16[4,32,4096]{2,1,0:T(8,128)(2,1)} custom-call(bf16[4,3,32,4096]{3,2,1,0:T(8,128)(2,1)} %bitcast.7, f32[512,256]{1,0:T(8,128)} %impulse_ref.1, f32[2,128]{1,0:T(2,128)} %bitcast.9, bf16[1024,512]{1,0:T(8,128)(2,1)} %constant.4.clone.high_hbm, bf16[1024,512]{1,0:T(8,128)(2,1)} %constant.5.clone.low_hbm), custom_call_target="tpu_custom_call" | custom-call | tf_op jit(solution)/shard_map/pallas_call | solution.py:340
  52.5 2.8 %fusion = bf16[4,32,4096]{2,1,0:T(8,128)(2,1)} fusion(bf16[4,32,4096]{2,1,0:T(8,128)(2,1)} %shard_map.55, bf16[4,3,32,4096]{3,2,1,0:T(8,128)(2,1)} %bitcast.8), kind=kLoop, calls=%fused_computation.1 | loop fusion | flops 2097152 | bytes 3145728 | tf_op jit(solution)/shard_map/convert_element_type | solution.py:371

commit v3 on v2

--- a/solution.py
+++ b/solution.py
@@ -116,9 +116,9 @@
 def mixer_kernel(
     ctx_size, ch_size,
     proj_ref, impulse_ref, skip_ref, high_hbm, low_hbm,
-    conv_ref,
-    high_ref, low_ref,    kv, mixed, received, result, lags, coef, back_high, back_low, sum_high, sum_low,
-    load_sem, table_sems, lag_sems, out_send, out_recv, home_send, home_recv,
+    gated_ref,
+    high_ref, low_ref,    kv, gate, conv_ref, mixed, received, result, lags, coef, back_high, back_low, sum_high, sum_low,
+    load_sem, gate_sem, store_sem, table_sems, lag_sems, out_send, out_recv, home_send, home_recv,
 ):
     seqs, _, tokens, _ = proj_ref.shape
     span = impulse_ref.shape[0]
@@ -159,6 +159,7 @@
 
     for s in range(seqs):
         load(s).start()
+    gate_load = pltpu.make_async_copy(proj_ref.at[:, 0], gate, gate_sem)
     own_lag = pltpu.make_async_copy(
         impulse_ref.at[:, pl.ds(pl.multiple_of(y * LANES, LANES), LANES)], lags.at[y], lag_sems.at[0]
     )
@@ -169,6 +170,7 @@
     ]
     for table in tables:
         table.start()
+    gate_load.start()
 
     def multiply(s, carry):
         load(s).wait()
@@ -315,15 +317,31 @@
 
     lax.fori_loop(0, groups, send_home, 0)
 
+    def store(s):
+        return pltpu.make_async_copy(kv.at[s, 0], gated_ref.at[s], store_sem.at[s])
+
+    def apply_gate(s, carry):
+        kv[s, 0] = (gate[s].astype(jnp.float32) * conv_ref[s].astype(jnp.float32)).astype(jnp.bfloat16)
+        store(s).start()
+        return carry
+
     def drain(g, carry):
         sent = received.at[group(g), pl.ds(0, (count - 1) * tokens), :]
         home = conv_ref.at[group(g)]
         pltpu.make_async_copy(sent, sent, out_send.at[g]).wait()
         pltpu.make_async_copy(sent, sent, home_send.at[g]).wait()
         pltpu.make_async_copy(home, home, home_recv.at[g]).wait()
-        return carry
-
+        lax.fori_loop(g * several, (g + 1) * several, apply_gate, carry)
+        return carry
+
+    gate_load.wait()
     lax.fori_loop(0, groups, drain, 0)
+
+    def finish(s, carry):
+        store(s).wait()
+        return carry
+
+    lax.fori_loop(0, seqs, finish, 0)
 
 
 def split_body(projections, impulse, skip_gain):
@@ -337,7 +355,7 @@
     hbm = pl.BlockSpec(memory_space=pltpu.HBM)
     vmem = pl.BlockSpec(memory_space=pltpu.VMEM)
     bf16, f32 = jnp.bfloat16, jnp.float32
-    convolved = pl.pallas_call(
+    return pl.pallas_call(
         functools.partial(mixer_kernel, ctx_size, ch_size),
         out_shape=jax.ShapeDtypeStruct((seqs, tokens, width), bf16),
         in_specs=[hbm, hbm, vmem, hbm, hbm],
@@ -347,6 +365,8 @@
             pltpu.VMEM((2 * span, span), bf16),
             pltpu.VMEM((seqs, 2, tokens, width), bf16),
             pltpu.VMEM((seqs, tokens, width), bf16),
+            pltpu.VMEM((seqs, tokens, width), bf16),
+            pltpu.VMEM((seqs, tokens, width), bf16),
             pltpu.VMEM((seqs, length, LANES), bf16),
             pltpu.VMEM((seqs, length, LANES), bf16),
             pltpu.VMEM((2, span, LANES), f32),
@@ -356,6 +376,8 @@
             pltpu.VMEM((2 * span, 2 * LANES), bf16),
             pltpu.VMEM((2 * span, 2 * LANES), bf16),
             pltpu.SemaphoreType.DMA((seqs,)),
+            pltpu.SemaphoreType.DMA,
+            pltpu.SemaphoreType.DMA((seqs,)),
             pltpu.SemaphoreType.DMA((2,)),
             pltpu.SemaphoreType.DMA((3,)),
             pltpu.SemaphoreType.DMA((seqs,)),
@@ -367,8 +389,6 @@
             collective_id=0, has_side_effects=True, vmem_limit_bytes=60 * 1024 * 1024
         ),
     )(features, impulse, skip_gain.reshape(2, LANES), jnp.asarray(high), jnp.asarray(low))
-    gate = features[:, 0]
-    return (gate.astype(f32) * convolved.astype(f32)).astype(bf16)
 
 
 def body(projections, impulse, skip_gain):

time: 55.4 us -> 55.7 us (level)
  other arithmetic: 2.76 us -> 0 us
  local copies, waits for them, and re-layouts: 0 us -> 2.29 us
  Pallas kernels: 52.4 us -> 53.3 us
    convert_element_type x1 -> x0, other arithmetic: 2.76 us -> none  [split_body(): return (gate.astype(f32) * convolved.astype(f32)).astype(bf16)]
    unnamed x0 -> x1, local copies, waits for them, and re-layouts: none -> 2.29 us
    pallas_call x1, Pallas kernels: 52.4 us -> 53.3 us  [split_body(): pl.pallas_call(functools.partial(mixer_kernel, ctx_size, ch_size), out_sh...]
where the time goes in v3:
time: 55.7 us; the launch traced here: 55.6 us
  Pallas kernels  53.3 us (96%)
  local copies, waits for them, and re-layouts  2.29 us (4%)
    pallas_call x1, Pallas kernels, split_body(): pl.pallas_call(functools.partial(mixer_kernel, ctx_size, ch_size), out_sh...  53.3 us
    unnamed x1, local copies, waits for them, and re-layouts  2.29 us

profile of v3, /device:TPU:0, one launch (start us, length us, event | category | flops | bytes accessed | tf_op | source)
XLA Modules:
  0.0 55.6 jit_solution(6899035385409656414)
XLA Ops:
  0.0 53.3 %shard_map.55 = bf16[4,32,4096]{2,1,0:T(8,128)(2,1)} custom-call(bf16[4,3,32,4096]{3,2,1,0:T(8,128)(2,1)} %bitcast.2, f32[512,256]{1,0:T(8,128)} %impulse_ref.1, f32[2,128]{1,0:T(2,128)} %bitcast.3, bf16[1024,512]{1,0:T(8,128)(2,1)} %constant.4.clone.high_hbm, bf16[1024,512]{1,0:T(8,128)(2,1)} %constant.5.clone.low_hbm), custom_call_target="tpu_custom_call" | custom-call | tf_op jit(solution)/shard_map/pallas_call | solution.py:358
  53.3 2.3 %copy.7 = bf16[4,32,4096]{2,1,0:T(8,128)(2,1)} copy(bf16[4,32,4096]{2,1,0:T(8,128)(2,1)} %shard_map.55) | data formatting | bytes 2097152

commit v4 on v2

--- a/solution.py
+++ b/solution.py
@@ -364,9 +364,9 @@
             pltpu.SemaphoreType.DMA((seqs,)),
         ],
         compiler_params=pltpu.CompilerParams(
-            collective_id=0, has_side_effects=True, vmem_limit_bytes=60 * 1024 * 1024
+            collective_id=0, has_side_effects=True, vmem_limit_bytes=40 * 1024 * 1024
         ),
-    )(features, impulse, skip_gain.reshape(2, LANES), jnp.asarray(high), jnp.asarray(low))
+    )(*(pltpu.with_memory_space_constraint(x, pltpu.HBM) for x in (features, impulse, skip_gain.reshape(2, LANES), jnp.asarray(high), jnp.asarray(low))))
     gate = features[:, 0]
     return (gate.astype(f32) * convolved.astype(f32)).astype(bf16)
 

time: 55.4 us -> 55 us (level)
  no operation moved by 1% of the time
where the time goes in v4:
time: 55 us; the launch traced here: 54.8 us
  Pallas kernels  52.3 us (95%)
  other arithmetic  2.45 us (4%)
    pallas_call x1, Pallas kernels, split_body(): pl.pallas_call(functools.partial(mixer_kernel, ctx_size, ch_size), out_sh...  52.3 us
    convert_element_type x1, other arithmetic, split_body(): return (gate.astype(f32) * convolved.astype(f32)).astype(bf16)  2.45 us

profile of v4, /device:TPU:0, one launch (start us, length us, event | category | flops | bytes accessed | tf_op | source)
XLA Modules:
  0.0 54.8 jit_solution(15540399676322124754)
XLA Ops:
  0.0 52.3 %shard_map.55 = bf16[4,32,4096]{2,1,0:T(8,128)(2,1)S(1)} custom-call(bf16[4,3,32,4096]{3,2,1,0:T(8,128)(2,1)} %bitcast.7, f32[512,256]{1,0:T(8,128)} %impulse_ref.1, f32[2,128]{1,0:T(2,128)} %bitcast.9, bf16[1024,512]{1,0:T(8,128)(2,1)} %constant.4.clone.high_hbm, bf16[1024,512]{1,0:T(8,128)(2,1)} %constant.5.clone.low_hbm), custom_call_target="tpu_custom_call" | custom-call | tf_op jit(solution)/shard_map/pallas_call | solution.py:340
  52.3 2.5 %fusion = bf16[4,32,4096]{2,1,0:T(8,128)(2,1)} fusion(bf16[4,32,4096]{2,1,0:T(8,128)(2,1)S(1)} %shard_map.55, bf16[4,3,32,4096]{3,2,1,0:T(8,128)(2,1)} %bitcast.8), kind=kLoop, calls=%fused_computation.1 | loop fusion | flops 2097152 | bytes 3145728 | tf_op jit(solution)/shard_map/convert_element_type | solution.py:371
